TPU v7x, 32 devices: a whole 2x2x4 slice. The times are simulated.
32 devices in a mesh: groups: 2 (over x), seq: 16 (over z, y, core).
Axes of the slice: x: 2, y: 2, z: 4, core: 2. Of those that a mesh axis runs over, the one named last changes fastest.
Arguments:
- features: bfloat16 [3, 4096, 4096], P(None, ('groups', 'seq')), parts along dimension 1, may hold values from -6 to 6
- kernel: float32 [3, 3, 4096], replicated, may hold values from -3.5 to 3.5
- skip: float32 [4096], replicated, may hold values from -4 to 4
- residues: float32 [2, 16, 4096], replicated, may hold values from -3 to 3
- decay: float32 [16, 4096], replicated, may hold values from 9.765625e-05 to 0.041666667
- freq: float32 [16, 4096], replicated, may hold values from 0.001 to 0.5
- lengths: int32 [12], P('groups'), parts along dimension 0, may hold values from 1 to 1024, 2048 in all
Outputs:
- mixed: bfloat16 [4096, 4096], P(('groups', 'seq')), parts along dimension 0
There are 2 independent parts, one for each index of `groups`. A program takes and returns all parts, laid end to end along the dimension named above; an argument that names none is the same for every part. Nothing has to cross between parts.
Inputs may be any that keep to these rules, and one draw needn't show every extreme that they name: The lengths sum to 2048; the longest is exactly 1024.
All inputs are finite; a program needn't handle non-finite values.
Results may differ from a plain program's by a relative error of at most 0.0065.
Values may be sent and summed in bfloat16 or wider, within the bound.
No kernel may reach another device: no remote copies, remote signals or barrier semaphores. Data moves between devices by JAX's collectives and lax.ppermute only.
A program may use at most 192 MiB of HBM per device.

v0:
```python
import functools

import jax
import jax.numpy as jnp
from jax import lax
from jax.experimental import pallas as pl
from jax.experimental.pallas import tpu as pltpu
from jax.sharding import PartitionSpec as P

BLK = 16
LANE = 128
SUB = 8
TILE = 512
PITCH = 40
ROOM = 50
PIECE = 256
CHUNK = 512
UNROLL = 2
F32 = jnp.float32
BF16 = jnp.bfloat16


def exchange(block, distance):
    devices = range(lax.axis_size("seq"))
    return lax.ppermute(block, "seq", [(i, i ^ distance) for i in devices])


def row_iota(rows):
    return lax.broadcasted_iota(jnp.int32, (rows, LANE), 0)


def starts_of(lengths_ref, origin):
    starts, at = [], -origin
    for i in range(lengths_ref.shape[0]):
        starts.append(at)
        at = at + lengths_ref[i]
    return starts


def none_in(starts, first, beyond):
    hit = jnp.int32(0)
    for s in starts:
        hit = hit | ((s >= first) & (s < beyond)).astype(jnp.int32)
    return (1 - hit).astype(F32)


def block_flags(starts, count):
    return [none_in(starts, b * BLK, (b + 1) * BLK) for b in range(count)]


def shift_matrix(starts, tokens):
    t = lax.broadcasted_iota(jnp.int32, (tokens, tokens), 0)
    u = lax.broadcasted_iota(jnp.int32, (tokens, tokens), 1)
    here = jnp.zeros((tokens, tokens), jnp.bool_)
    before = jnp.zeros((tokens, tokens), jnp.bool_)
    for s in starts:
        here = here | (t == s)
        before = before | (t - 1 == s)
    one = jnp.where((u == t - 1) & ~here, 1.0, 0.0)
    two = jnp.where((u == t - 2) & ~(here | before), 1.0, 0.0)
    return jnp.concatenate([one, two], axis=0).astype(BF16)


def edge_flags(starts):
    return none_in(starts, 0, 1), none_in(starts, -1, 1), none_in(starts, 0, 2)


def short_filter(rows, halo, taps, shift_ref, edges):
    tokens, width = rows.shape
    moved = jnp.dot(shift_ref[...], rows, preferred_element_type=F32)
    behind, further = moved[:tokens], moved[tokens:]
    edge = halo.astype(F32)
    far, near = edge[0:1, :], edge[1:2, :]
    row = lax.broadcasted_iota(jnp.int32, (SUB, width), 0)
    top = behind[:SUB] + jnp.where(row == 0, near * edges[0], 0.0)
    behind = jnp.concatenate([top, behind[SUB:]], axis=0)
    top = further[:SUB] + jnp.where(row == 0, far * edges[1], jnp.where(row == 1, near * edges[2], 0.0))
    further = jnp.concatenate([top, further[SUB:]], axis=0)
    return taps[0:1, :] * rows.astype(F32) + taps[1:2, :] * behind + taps[2:3, :] * further


def lane_tile(tile):
    return pl.ds(pl.multiple_of(tile * LANE, LANE), LANE)


def cmul(a_re, a_im, b_re, b_im):
    return a_re * b_re - a_im * b_im, a_re * b_im + a_im * b_re


def column_sums(parts):
    row = lax.broadcasted_iota(jnp.int32, (SUB, LANE), 0)
    low = row < 4
    level = []
    for b in range(4):
        keep = jnp.where(low, parts[b], parts[b + 4])
        move = jnp.where(low, parts[b + 4], parts[b])
        level.append(keep + pltpu.roll(move, 4, 0))
    for step in (2, 1):
        clear = (row & step) == 0
        level = [
            jnp.where(
                clear,
                level[b] + pltpu.roll(level[b], SUB - step, 0),
                level[b + step] + pltpu.roll(level[b + step], step, 0),
            )
            for b in range(step)
        ]
    return level[0]


def rows_of(ref, h, lanes):
    return ref[pl.ds(h * SUB, SUB), lanes]


def half_lanes(mine, half, offset, size):
    core = lax.axis_index("seq") & 1
    core = core if mine else 1 - core
    return pl.ds(pl.multiple_of(core * half + offset, LANE), size)


def flag_rows(rounds):
    names = ["odd", "second", "even", "edge0", "edge1", "edge2"] + [("tree", i) for i in range(16)]
    names += [(kind, k) for k in range(1, rounds) for kind in ("upper", "enter", "whole")]
    return {name: i for i, name in enumerate(names)}


def prelude_kernel(lengths_ref, features_ref, streams_ref, shift_ref, last_ref, flags_ref, sems, *, rounds):
    size = streams_ref.shape[1] // sems.shape[1]
    copies = [
        pltpu.make_async_copy(
            features_ref.at[r, pl.ds(j * size, size), :], streams_ref.at[u, pl.ds(j * size, size), :], sems.at[u, j]
        )
        for u, r in enumerate((0, 2))
        for j in range(sems.shape[1])
    ]
    for copy in copies:
        copy.start()
    tokens = streams_ref.shape[1]
    place = lax.axis_index("seq")
    starts = starts_of(lengths_ref, place * tokens)
    t = row_iota(tokens)
    last = jnp.full((tokens, LANE), -1, jnp.int32)
    for s in starts:
        last = jnp.maximum(last, jnp.where(s <= (t | (BLK - 1)), s, -1))
    last_ref[...] = jnp.where(t >= last, 1.0, 0.0)
    shift_ref[...] = shift_matrix(starts, tokens)
    values = dict(zip(("edge0", "edge1", "edge2"), edge_flags(starts)))
    span, i = BLK, 0
    while span < tokens:
        for first in range(span, tokens, 2 * span):
            values["tree", i] = none_in(starts, first, first + span)
            i += 1
        span *= 2
    starts = starts_of(lengths_ref, 0)
    even, second = place & -2, place | 1
    values["odd"] = (place & 1).astype(F32)
    values["even"] = none_in(starts, even * tokens, (even + 1) * tokens)
    values["second"] = none_in(starts, second * tokens, (second + 1) * tokens)
    for k in range(1, rounds):
        distance = 1 << k
        upper = ((place >> k) & 1).astype(F32)
        group = (place >> k) << k
        later = group | distance
        values["upper", k] = upper
        values["enter", k] = upper * none_in(starts, group * tokens, even * tokens)
        values["whole", k] = none_in(starts, later * tokens, (later + distance) * tokens)
    for name, row in flag_rows(rounds).items():
        if name in values:
            flags_ref[row : row + 1, :] = jnp.full((1, CHUNK), values[name], F32)
    for copy in copies:
        copy.wait()


def tables_kernel(decay_ref, freq_ref, residues_ref, pole_ref, coef_ref):
    modes, width = decay_ref.shape

    @pl.loop(0, width // CHUNK)
    def _(part):
        lanes = pl.ds(pl.multiple_of(part * CHUNK, LANE), CHUNK)
        decay, x = decay_ref[:, lanes], freq_ref[:, lanes]
        fade = jnp.exp(-decay)
        q = x * x
        sine = x * (1 + q * (-1 / 6 + q * (1 / 120 + q * (-1 / 5040 + q * (1 / 362880)))))
        cosine = 1 + q * (-1 / 2 + q * (1 / 24 + q * (-1 / 720 + q * (1 / 40320 - q * (1 / 3628800)))))
        store(pole_ref, lanes, (fade * cosine, fade * sine))
        d = 2 * decay
        scale = jnp.sqrt(d * (1 - d * (1 / 2 - d * (1 / 6 - d * (1 / 24 - d * (1 / 120 - d * (1 / 720)))))))
        store(coef_ref, lanes, (residues_ref[0, :, lanes] * scale, residues_ref[1, :, lanes] * scale))


def front_kernel(streams_ref, halo_ref, taps_ref, pole_ref, shift_s, last_s, flags_ref, z_ref, e_ref, end_ref, z_s, *, mine):
    tokens, half = z_ref.shape
    count = tokens // BLK
    modes = pole_ref.shape[0] // 2
    halves = modes // SUB
    wide = TILE
    rows_at = flag_rows(1)

    def flag(name, size):
        return flags_ref[rows_at[name] : rows_at[name] + 1, 0:size]

    edges = [flag(name, PIECE) for name in ("edge0", "edge1", "edge2")]

    @pl.loop(0, half // wide)
    def _(j):
        def gated(i, size):
            at = pl.ds(pl.multiple_of(j * wide + i * LANE, LANE), size)
            lanes = half_lanes(mine, half, j * wide + i * LANE, size)
            conv0, conv2 = (
                short_filter(streams_ref[u, :, lanes], halo_ref[r, :, lanes], taps_ref[r, :, lanes], shift_s, edges)
                for u, r in enumerate((0, 2))
            )
            z = (conv0 * conv2).astype(BF16)
            z_ref[:, at] = z
            for v in range(size // LANE):
                z_s[i + v, 0:tokens, :] = z[:, v * LANE : (v + 1) * LANE].astype(F32) * last_s[...]

        def states(i):
            at = pl.ds(pl.multiple_of(j * wide + i * LANE, LANE), LANE)
            lanes = half_lanes(mine, half, j * wide + i * LANE, LANE)
            z_i = z_s.at[i]
            p_re = [rows_of(pole_ref, h, lanes) for h in range(halves)]
            p_im = [rows_of(pole_ref, halves + h, lanes) for h in range(halves)]
            pow_re, pow_im = list(p_re), list(p_im)
            e_re, e_im = [], []
            for b in range(count):
                now = z_i[pl.ds(b * BLK + BLK - 1, SUB, stride=0), :]
                prev = z_i[pl.ds(b * BLK + BLK - 2, SUB, stride=0), :]
                e_re.append([now + p_re[h] * prev for h in range(halves)])
                e_im.append([p_im[h] * prev for h in range(halves)])
            for k in range(2, BLK):
                for h in range(halves):
                    pow_re[h], pow_im[h] = cmul(pow_re[h], pow_im[h], p_re[h], p_im[h])
                for b in range(count):
                    now = z_i[pl.ds(b * BLK + BLK - 1 - k, SUB, stride=0), :]
                    for h in range(halves):
                        e_re[b][h] = e_re[b][h] + pow_re[h] * now
                        e_im[b][h] = e_im[b][h] + pow_im[h] * now
            for h in range(halves):
                rows, rows_im = pl.ds(h * SUB, SUB), pl.ds(modes + h * SUB, SUB)
                for b in range(count):
                    e_ref[b, rows, at] = e_re[b][h]
                    e_ref[b, rows_im, at] = e_im[b][h]
                gate = cmul(pow_re[h], pow_im[h], p_re[h], p_im[h])
                level = [(e_re[b][h], e_im[b][h]) for b in range(count)]
                step = 0
                while len(level) > 1:
                    pairs = range(0, len(level), 2)
                    level = [
                        advance(gate, flag(("tree", step + i // 2), LANE), level[i], level[i + 1]) for i in pairs
                    ]
                    step += len(pairs)
                    gate = cmul(*gate, *gate)
                end_ref[rows, at] = level[0][0].astype(BF16)
                end_ref[rows_im, at] = level[0][1].astype(BF16)

        lane_tiles = wide // LANE
        gated(0, PIECE)
        for i in range(lane_tiles):
            following = (i // (PIECE // LANE) + 1) * (PIECE // LANE)
            if i % (PIECE // LANE) == 0 and following < lane_tiles:
                gated(following, PIECE)
            states(i)


def middle_kernel(lengths_ref, features_ref, halo_ref, taps_ref, z_ref, skip_ref, pole_ref,
                  coef_ref, base_ref, gain_ref, first_s, part_s, z_s, filt_s, acc_s, shift_s, piece_s, *, mine):
    tokens, half = z_ref.shape
    count = tokens // BLK
    modes = pole_ref.shape[0] // 2
    halves = modes // SUB
    starts = starts_of(lengths_ref, lax.axis_index("seq") * tokens)
    edges = edge_flags(starts)
    t = row_iota(tokens)
    t0 = t & (-BLK)
    piece = jnp.zeros((tokens, LANE), jnp.int32)
    opened = jnp.zeros((tokens, LANE), jnp.bool_)
    for s in starts:
        piece = piece + jnp.where((s > t0) & (s <= t), 1, 0)
        opened = opened | ((s >= t0) & (s <= t))
    part_s[...] = piece.astype(F32)
    first_s[...] = jnp.where(opened, 0.0, 1.0)
    shift_s[...] = shift_matrix(starts, tokens)

    pieces = []
    for b in range(count):
        inside = jnp.int32(1)
        for s in starts:
            inside = inside + ((s > b * BLK) & (s < (b + 1) * BLK)).astype(jnp.int32)
        pieces.append(inside)
    wide = TILE

    @pl.loop(0, half // wide)
    def _(part):
        here = pl.ds(pl.multiple_of(part * wide, LANE), wide)
        lanes = half_lanes(mine, half, part * wide, wide)
        conv1 = short_filter(features_ref[1, :, lanes], halo_ref[1, :, lanes], taps_ref[1, :, lanes], shift_s, edges)
        base_ref[:, here] = conv1
        for i in range(wide // LANE):
            inner = pl.ds(pl.multiple_of(part * wide + i * LANE, LANE), LANE)
            gain_ref[:, inner] = conv1[:, i * LANE : (i + 1) * LANE] * first_s[...]

    @pl.loop(0, half // LANE)
    def _(tile):
        here = lane_tile(tile)
        lanes = half_lanes(mine, half, tile * LANE, LANE)
        p_re = [rows_of(pole_ref, h, lanes) for h in range(halves)]
        p_im = [rows_of(pole_ref, halves + h, lanes) for h in range(halves)]
        q_re = [rows_of(coef_ref, h, lanes) for h in range(halves)]
        q_im = [rows_of(coef_ref, halves + h, lanes) for h in range(halves)]
        filt_s[pl.ds(0, BLK), :] = jnp.zeros((BLK, LANE), F32)
        for group in range(BLK // SUB):
            parts = []
            for k in range(SUB):
                parts.append(sum(q_re[1:], q_re[0]))
                for h in range(halves):
                    q_re[h], q_im[h] = cmul(q_re[h], q_im[h], p_re[h], p_im[h])
            filt_s[pl.ds(BLK + group * SUB, SUB), :] = column_sums(parts).astype(BF16).astype(F32)
        z = z_ref[:, here].astype(F32)
        z_s[0:tokens, :] = z
        acc = skip_ref[:, lanes] * z
        sums = [[acc[b * BLK + r * SUB : b * BLK + (r + 1) * SUB] for r in range(BLK // SUB)] for b in range(count)]
        for s in range(BLK):
            firsts = range(s // SUB, BLK // SUB)
            columns = {r: filt_s[pl.ds(BLK - s + r * SUB, SUB), :] for r in firsts}
            for b in range(count):
                value = z_s[pl.ds(b * BLK + s, SUB, stride=0), :]
                for r in firsts:
                    sums[b][r] = sums[b][r] + columns[r] * value
        for b in range(count):
            for r in range(BLK // SUB):
                acc_s[pl.ds(b * BLK + r * SUB, SUB), :] = sums[b][r]

        for b in range(count):
            @pl.when(pieces[b] > 1)
            def _(b=b):
                rows = pl.ds(b * BLK, BLK)
                acc_s[rows, :] = skip_ref[:, lanes] * z_s[rows, :]

                def one_piece(q, carry):
                    member = part_s[rows, :] == q.astype(F32)
                    piece_s[...] = jnp.where(member, z_s[rows, :], 0.0)
                    total = jnp.zeros((BLK, LANE), F32)
                    for s in range(BLK):
                        total = total + filt_s[pl.ds(BLK - s, BLK), :] * piece_s[pl.ds(s, 1), :]
                    acc_s[rows, :] = acc_s[rows, :] + jnp.where(member, total, 0.0)
                    return carry

                lax.fori_loop(0, pieces[b], one_piece, 0)

        base_ref[:, here] = base_ref[:, here] * acc_s[...]


def prepare_kernel(lengths_ref, e_ref, pole_ref, coef_ref, table_ref, local_ref, reach_ref, turn_s, *, mine):
    count, packed, half = e_ref.shape
    modes = packed // 2
    halves = modes // SUB
    starts = starts_of(lengths_ref, lax.axis_index("seq") * count * BLK)
    flags = block_flags(starts, count)
    pitch = turn_s.shape[0] // BLK

    @pl.loop(0, half // LANE)
    def _(tile):
        here = lane_tile(tile)
        lanes = half_lanes(mine, half, tile * LANE, LANE)
        for h in range(halves):
            rows, rows_im = pl.ds(h * SUB, SUB), pl.ds(modes + h * SUB, SUB)
            p = pole_ref[rows, lanes], pole_ref[rows_im, lanes]
            q = coef_ref[rows, lanes], coef_ref[rows_im, lanes]
            for k in range(BLK):
                q = cmul(*q, *p)
                turn_s[pl.ds(k * pitch + h * SUB, SUB), :] = q[0]
                turn_s[pl.ds(k * pitch + modes + h * SUB, SUB), :] = -q[1]
            gate = p
            for _ in range(BLK.bit_length() - 1):
                gate = cmul(*gate, *gate)
            zero = jnp.zeros((SUB, LANE), F32)
            state, reach = (zero, zero), (zero + 1.0, zero)
            for b in range(count):
                local_ref[b, rows, here], local_ref[b, rows_im, here] = state
                reach_ref[b, rows, here], reach_ref[b, rows_im, here] = reach
                if b < count - 1:
                    state = advance(gate, flags[b], state, (e_ref[b, rows, here], e_ref[b, rows_im, here]))
                    reach = tuple(flags[b] * x for x in cmul(*gate, *reach))
        for m in range(packed):
            for r in range(BLK // SUB):
                table_ref[m, pl.ds(r * SUB, SUB), here] = turn_s[pl.ds(r * SUB * pitch + m, SUB, stride=pitch), :]


def split(ref, lanes, *lead):
    modes = ref.shape[-2] // 2
    packed = ref[(*lead, slice(None), lanes)].astype(F32)
    return packed[:modes], packed[modes:]


def store(ref, lanes, pair):
    modes = ref.shape[-2] // 2
    ref[0:modes, lanes] = pair[0].astype(ref.dtype)
    ref[modes : 2 * modes, lanes] = pair[1].astype(ref.dtype)


def advance(gate, flag, state, addend):
    re, im = cmul(*gate, *state)
    return addend[0] + flag * re, addend[1] + flag * im


def choose(flag, a, b):
    return tuple(jnp.where(flag, x, y) for x, y in zip(a, b))


def first_kernel(kept_ref, came_ref, pole_ref, flags_ref, total_ref, send_ref, gate_ref, *, tokens):
    half = kept_ref.shape[1]
    rows_at = flag_rows(1)
    shape = kept_ref.shape[0] // 2, CHUNK

    @pl.loop(0, half // CHUNK)
    def _(part):
        def flag(name):
            return jnp.broadcast_to(flags_ref[rows_at[name] : rows_at[name] + 1, :], shape)

        lanes = pl.ds(pl.multiple_of(part * CHUNK, LANE), CHUNK)
        kept, came = split(kept_ref, lanes), split(came_ref, lanes)
        gate = split(pole_ref, half_lanes(True, half, part * CHUNK, CHUNK))
        odd = flag("odd") > 0.5
        reach = 1
        while reach < tokens:
            gate = cmul(*gate, *gate)
            reach *= 2
        total = advance(gate, flag("second"), choose(odd, came, kept), choose(odd, kept, came))
        store(total_ref, lanes, total)
        store(send_ref, lanes, total)
        store(gate_ref, lanes, gate)


def round_kernel(total_ref, met_ref, flags_ref, *refs, k, rounds):
    rows_at = flag_rows(rounds)
    shape = met_ref.shape[0] // 2, CHUNK

    @pl.loop(0, met_ref.shape[1] // CHUNK)
    def _(part):
        def flag(name):
            return jnp.broadcast_to(flags_ref[rows_at[name] : rows_at[name] + 1, :], shape)

        lanes = pl.ds(pl.multiple_of(part * CHUNK, LANE), CHUNK)
        rest = list(refs)
        met, total = split(met_ref, lanes), split(total_ref, lanes)
        power = split(rest.pop(0), lanes)
        enter = flag(("enter", k))
        if k == 1:
            prefix = tuple(enter * x for x in met)
        else:
            before, prefix = split(rest.pop(0), lanes), split(rest.pop(0), lanes)
            prefix = advance(before, enter, met, prefix)
        if k < rounds - 1:
            total_out, send_ref, power_out, before_out, prefix_out = rest
            upper = flag(("upper", k)) > 0.5
            power = cmul(*power, *power)
            total = advance(power, flag(("whole", k)), choose(upper, met, total), choose(upper, total, met))
            store(total_out, lanes, total)
            store(send_ref, lanes, total)
            store(prefix_out, lanes, prefix)
            store(power_out, lanes, power)
            if k == 1:
                before = choose(upper, power, (jnp.ones_like(met[0]), jnp.zeros_like(met[0])))
            else:
                before = choose(upper, cmul(*before, *power), before)
            store(before_out, lanes, before)
        else:
            gate_ref, kept_ref, came_ref, own_ref, send_ref = rest
            odd = flag("odd") > 0.5
            kept, came = split(kept_ref, lanes), split(came_ref, lanes)
            beyond = advance(split(gate_ref, lanes), flag("even"), prefix, choose(odd, came, kept))
            store(own_ref, lanes, choose(odd, beyond, prefix))
            store(send_ref, lanes, choose(odd, prefix, beyond))


def back_kernel(entry_ref, table_ref, local_ref, reach_ref, base_ref, gain_ref, *refs, mine):
    out_hbm, out_ref, state_s, sems = refs[-4:]
    tokens, half = out_ref.shape
    width = TILE
    count, packed, _ = local_ref.shape
    modes = packed // 2
    halves = modes // SUB
    def one_tile(tile, state_s):
        lanes = here = lane_tile(tile)
        entry = entry_ref[:, here].astype(F32)
        for h in range(halves):
            rows, rows_im = pl.ds(h * SUB, SUB), pl.ds(modes + h * SUB, SUB)
            first = entry[h * SUB : (h + 1) * SUB], entry[modes + h * SUB : modes + (h + 1) * SUB]
            for b in range(count):
                state = first
                if b:
                    state = cmul(reach_ref[b, rows, here], reach_ref[b, rows_im, here], *first)
                    state = state[0] + local_ref[b, rows, here], state[1] + local_ref[b, rows_im, here]
                state_s[pl.ds(b * packed + h * SUB, SUB), :] = state[0]
                state_s[pl.ds(b * packed + modes + h * SUB, SUB), :] = state[1]
        sums = [[None] * (BLK // SUB) for _ in range(count)]
        for m in range(packed):
            turn = [table_ref[m, pl.ds(r * SUB, SUB), here] for r in range(BLK // SUB)]
            for b in range(count):
                state = state_s[pl.ds(b * packed + m, SUB, stride=0), :]
                for r in range(BLK // SUB):
                    term = turn[r] * state
                    sums[b][r] = term if m == 0 else sums[b][r] + term
        for b in range(count):
            rows = pl.ds(b * BLK, BLK)
            carried = jnp.concatenate(sums[b], axis=0)
            out_ref[rows, lanes] = (base_ref[rows, here] + gain_ref[rows, here] * carried).astype(BF16)

    def leaving(j):
        lanes = half_lanes(mine, half, j * width, width)
        here = pl.ds(pl.multiple_of(j * width, LANE), width)
        return pltpu.make_async_copy(out_ref.at[:, here], out_hbm.at[:, lanes], sems.at[j])

    @pl.loop(0, half // width)
    def _(j):
        @pl.loop(0, width // LANE // state_s.shape[0])
        def _(step):
            for v in range(state_s.shape[0]):
                one_tile(j * (width // LANE) + step * state_s.shape[0] + v, state_s.at[v])

        leaving(j).start()

    for j in range(half // width):
        leaving(j).wait()


def per_device(features, kernel, skip, residues, decay, freq, lengths):
    tokens = features.shape[1]
    modes, width = decay.shape
    half = width // 2
    count = tokens // BLK
    n = lax.axis_size("seq")
    place = lax.axis_index("seq")
    core = place % 2
    rounds = n.bit_length() - 1

    rim = features[:, tokens - 2 :, :]
    halo = lax.ppermute(rim, "seq", [(i, (i + 1) % n) for i in range(n)])

    params = pltpu.CompilerParams(vmem_limit_bytes=16 * 1024 * 1024)
    roomy = pltpu.CompilerParams(vmem_limit_bytes=ROOM * 1024 * 1024)
    plane = pltpu.VMEM((tokens, LANE), F32)
    shifts = pltpu.VMEM((2 * tokens, tokens), BF16)
    whole = pl.BlockSpec(memory_space=pltpu.VMEM)

    def call(body, args, outs, name, scratch=(), cost=0.8e9, ragged=False, spec=whole, limit=params):
        return pl.pallas_call(
            body,
            grid_spec=pltpu.PrefetchScalarGridSpec(
                num_scalar_prefetch=int(ragged), grid=(), in_specs=[spec] * len(args), out_specs=[whole] * len(outs),
                scratch_shapes=scratch,
            ),
            out_shape=[jax.ShapeDtypeStruct(*o) for o in outs],
            compiler_params=limit, name=name,
            cost_estimate=pl.CostEstimate(flops=int(cost), bytes_accessed=1 << 20, transcendentals=0),
        )(*((lengths,) if ragged else ()), *args)

    packed = 2 * modes
    state, sent = ((packed, half), F32), ((packed, half), BF16)
    blocks, plain = ((count, packed, half), F32), ((tokens, half), F32)

    flag_count = -(-len(flag_rows(rounds)) // SUB) * SUB
    streams, shift, last_mask, flags = call(
        functools.partial(prelude_kernel, rounds=rounds), (features,),
        (((2, tokens, width), BF16), ((2 * tokens, tokens), BF16), ((tokens, LANE), F32), ((flag_count, CHUNK), F32)),
        "prelude", [pltpu.SemaphoreType.DMA((2, 4))], ragged=True, spec=pl.BlockSpec(memory_space=pl.ANY), limit=roomy,
        cost=1.2e9,
    )

    table = ((packed, width), F32)
    pole, coef = call(tables_kernel, (decay, freq, residues), (table, table), "tables", cost=0.5e9)

    def front(mine):
        return call(
            functools.partial(front_kernel, mine=mine), (streams, halo, kernel, pole, shift, last_mask, flags),
            (((tokens, half), BF16), blocks, sent), "front", [pltpu.VMEM((TILE // LANE, tokens + SUB, LANE), F32)], cost=5e9,
        )

    def middle(mine, z):
        return call(
            functools.partial(middle_kernel, mine=mine), (features, halo, kernel, z, skip[None], pole, coef),
            (plain, plain), "middle", [plane, plane, pltpu.VMEM((tokens + SUB, LANE), F32), pltpu.VMEM((2 * BLK, LANE), F32), plane, shifts, pltpu.VMEM((BLK, LANE), F32)], cost=5e9, ragged=True,
        )

    def prepare(mine, e):
        return call(
            functools.partial(prepare_kernel, mine=mine), (e, pole, coef),
            (((packed, BLK, half), F32), blocks, blocks), "prepare", [pltpu.VMEM((BLK * PITCH, LANE), F32)], cost=2.5e9, ragged=True,
        )

    def back(mine, args, out):
        specs = [whole] * len(args)
        if out is not None:
            args, specs = args + (out,), specs + [pl.BlockSpec(memory_space=pl.ANY)]

        return pl.pallas_call(
            functools.partial(back_kernel, mine=mine),
            in_specs=specs, out_specs=pl.BlockSpec(memory_space=pl.ANY),
            out_shape=jax.ShapeDtypeStruct((tokens, width), BF16),
            scratch_shapes=[pltpu.VMEM((tokens, half), BF16), pltpu.VMEM((UNROLL, count * packed + SUB, LANE), F32),
                            pltpu.SemaphoreType.DMA((half // TILE,))],
            input_output_aliases={} if out is None else {len(args) - 1: 0},
            compiler_params=params, name="back",
            cost_estimate=pl.CostEstimate(flops=3_500_000_000, bytes_accessed=1 << 20, transcendentals=0),
        )(*args)

    z_other, e_other, end_other = front(False)
    came = exchange(end_other, 1)
    z_own, e_own, end_own = front(True)
    total, send, gate = call(
        functools.partial(first_kernel, tokens=tokens), (end_own, came, pole, flags), (state, sent, state), "first"
    )
    power, carry = gate, ()
    jobs = [lambda z: middle(True, z), lambda z: middle(False, z), lambda es: (*prepare(True, es[0]), *prepare(False, es[1]))]
    inputs = [z_own, z_other, (e_own, e_other)]
    ready = []
    for k in range(1, rounds):
        last = k == rounds - 1
        met = exchange(send, 1 << k)
        for job, operand in [(jobs.pop(0), inputs.pop(0)) for _ in range(len(jobs) if last else min(1, len(jobs)))]:
            operand, send = lax.optimization_barrier((operand, send))
            met, done = lax.optimization_barrier((met, job(operand)))
            ready.append(done)
        body = functools.partial(round_kernel, k=k, rounds=rounds)
        args = (total, met, flags, power, *carry)
        if last:
            own, send = call(body, args + (gate, end_own, came), (state, sent), "round")
        else:
            total, send, power, *carry = call(body, args, (state, sent, state, state, state), "round")
    other = exchange(send, 1)
    out = back(True, (own, *ready[2][:3], *ready[0]), None)
    return back(False, (other, *ready[2][3:], *ready[1]), out)


def solution(mesh):
    return jax.shard_map(
        per_device,
        mesh=mesh,
        in_specs=(P(None, ("groups", "seq"), None), P(), P(), P(), P(), P(), P("groups")),
        out_specs=P(("groups", "seq"), None),
        check_vma=False,
    )
```

profile of v0, /device:TPU:1, one launch (start us, length us, event | category | flops | bytes accessed | tf_op | source)
XLA Modules:
  0.0 45.4 jit_solution(2080155486704622141)
XLA Ops:
  0.0 1.0 %slice.3 = bf16[3,2,4096]{2,1,0:T(2,128)(2,1)S(1)} slice(bf16[3,128,4096]{2,1,0:T(8,128)(2,1)} %features_ref.5), slice={[0:3], [126:128], [0:4096]} | slice | bytes 98304 | tf_op jit(solution)/shard_map/slice | solution.py:538
  1.0 2.7 %collective-permute-start = (bf16[3,2,4096]{2,1,0:T(2,128)(2,1)S(1)}, bf16[3,2,4096]{2,1,0:T(2,128)(2,1)S(1)}, u32[]{:S(2)}, u32[]{:S(2)}) collective-permute-start(bf16[3,2,4096]{2,1,0:T(2,128)(2,1)S(1)} %slice.3), channel_id=1, source_target_pairs={{0,1},{1,2},{2,3},{3,4},{4,5},{5,6},{6,7},{7,8},{8,9},{9,10},{10,1... | collective-permute-start | bytes 147464 | tf_op jit(solution)/shard_map/ppermute | solution.py:539
  3.7 0.7 %copy-done.6 = s32[6]{0:T(128)S(1)} copy-done((s32[6]{0:T(128)S(1)}, s32[6]{0:T(128)}, u32[]{:S(2)}) %copy-start.6) | copy-done | bytes 48
  4.4 2.1 %prelude.1 = (bf16[2,128,4096]{2,1,0:T(8,128)(2,1)S(1)}, bf16[256,128]{1,0:T(8,128)(2,1)S(1)}, f32[128,128]{1,0:T(8,128)S(1)}, f32[32,512]{1,0:T(8,128)S(1)}) custom-call(s32[6]{0:T(128)S(1)} %copy-done.6, bf16[3,128,4096]{2,1,0:T(8,128)(2,1)} %features_ref.5), custom_call_target="tpu_custom_call" | custom-call | flops 1200000000 | bytes 1048576 | tf_op jit(solution)/shard_map/prelude/pallas_call | solution.py:548
  6.5 0.5 %tables.1 = (f32[32,4096]{1,0:T(8,128)S(1)}, f32[32,4096]{1,0:T(8,128)S(1)}) custom-call(f32[16,4096]{1,0:T(8,128)S(1)} %copy-done.2, f32[16,4096]{1,0:T(8,128)S(1)} %copy-done.3, f32[2,16,4096]{2,1,0:T(8,128)S(1)} %copy-done.1), custom_call_target="tpu_custom_call" | custom-call | flops 500000000 | bytes 1048576 | tf_op jit(solution)/shard_map/tables/pallas_call | solution.py:548
  7.0 4.2 %front.3 = (bf16[128,2048]{1,0:T(8,128)(2,1)S(1)}, f32[8,32,2048]{2,1,0:T(8,128)S(1)}, bf16[32,2048]{1,0:T(8,128)(2,1)S(1)}) custom-call(bf16[2,128,4096]{2,1,0:T(8,128)(2,1)S(1)} %get-tuple-element.59.streams_ref, bf16[3,2,4096]{2,1,0:T(2,128)(2,1)S(1)} %collective-permute-done.halo_ref, f32[3,3,4096]{2,1,0:T(4,128)S(1)} %copy-done.4, ...), custom_call_target="tpu_custom_call" | custom-call | flops 5000000000 | bytes 1048576 | tf_op jit(solution)/shard_map/front/pallas_call | solution.py:548
  11.3 1.4 %collective-permute-start.1 = (bf16[32,2048]{1,0:T(8,128)(2,1)S(1)}, bf16[32,2048]{1,0:T(8,128)(2,1)S(1)}, u32[]{:S(2)}, u32[]{:S(2)}) collective-permute-start(bf16[32,2048]{1,0:T(8,128)(2,1)S(1)} %get-tuple-element.65), channel_id=1, source_target_pairs={{0,1},{1,0},{2,3},{3,2},{4,5},{5,4},{6,7},{7,6},{8,9},{9,8},{10,11... | collective-permute-start | bytes 393224 | tf_op jit(solution)/shard_map/ppermute | solution.py:25
  12.7 4.2 %front.2 = (bf16[128,2048]{1,0:T(8,128)(2,1)S(1)}, f32[8,32,2048]{2,1,0:T(8,128)S(1)}, bf16[32,2048]{1,0:T(8,128)(2,1)S(1)}) custom-call(bf16[2,128,4096]{2,1,0:T(8,128)(2,1)S(1)} %get-tuple-element.59.streams_ref, bf16[3,2,4096]{2,1,0:T(2,128)(2,1)S(1)} %collective-permute-done.halo_ref, f32[3,3,4096]{2,1,0:T(4,128)S(1)} %copy-done.4, ...), custom_call_target="tpu_custom_call" | custom-call | flops 5000000000 | bytes 1048576 | tf_op jit(solution)/shard_map/front/pallas_call | solution.py:548
  16.9 0.3 first.1
  17.2 0.1 collective-permute-start.2
  17.3 0.3 copy-done.5
  17.6 5.0 %middle.2 = (f32[128,2048]{1,0:T(8,128)S(1)}, f32[128,2048]{1,0:T(8,128)S(1)}) custom-call(s32[6]{0:T(128)S(1)} %copy-done.6, bf16[3,128,4096]{2,1,0:T(8,128)(2,1)S(1)} %copy-done, bf16[3,2,4096]{2,1,0:T(2,128)(2,1)S(1)} %collective-permute-done.halo_ref, f32[3,3,4096]{2,1,0:T(4,128)S(1)} %copy-done.4, bf16[128,2048]{1,0:T(8,128)(2,1)S(1)} %get-tuple-element.69.z_ref, ...), custom_call_target="tpu_custom_call" | custom-call | flops 5000000000 | bytes 1048576 | tf_op jit(solution)/shard_map/middle/pallas_call | solution.py:548
  22.7 0.2 round.3
  22.8 0.2 collective-permute-start.3
  23.0 5.0 %middle.3 = (f32[128,2048]{1,0:T(8,128)S(1)}, f32[128,2048]{1,0:T(8,128)S(1)}) custom-call(s32[6]{0:T(128)S(1)} %copy-done.6, bf16[3,128,4096]{2,1,0:T(8,128)(2,1)S(1)} %copy-done, bf16[3,2,4096]{2,1,0:T(2,128)(2,1)S(1)} %collective-permute-done.halo_ref, f32[3,3,4096]{2,1,0:T(4,128)S(1)} %copy-done.4, bf16[128,2048]{1,0:T(8,128)(2,1)S(1)} %get-tuple-element.78.z_ref, ...), custom_call_target="tpu_custom_call" | custom-call | flops 5000000000 | bytes 1048576 | tf_op jit(solution)/shard_map/middle/pallas_call | solution.py:548
  28.0 0.2 round.4
  28.3 0.7 %collective-permute-start.4 = (bf16[32,2048]{1,0:T(8,128)(2,1)S(1)}, bf16[32,2048]{1,0:T(8,128)(2,1)S(1)}, u32[]{:S(2)}, u32[]{:S(2)}) collective-permute-start(bf16[32,2048]{1,0:T(8,128)(2,1)S(1)} %get-tuple-element.86), channel_id=1, source_target_pairs={{0,8},{1,9},{2,10},{3,11},{4,12},{5,13},{6,14},{7,15},{8,0},{9,1},... | collective-permute-start | bytes 393224 | tf_op jit(solution)/shard_map/ppermute | solution.py:25
  28.9 2.5 %prepare.2 = (f32[32,16,2048]{2,1,0:T(8,128)S(1)}, f32[8,32,2048]{2,1,0:T(8,128)S(1)}, f32[8,32,2048]{2,1,0:T(8,128)S(1)}) custom-call(s32[6]{0:T(128)S(1)} %copy-done.6, f32[8,32,2048]{2,1,0:T(8,128)S(1)} %get-tuple-element.89.e_ref, f32[32,4096]{1,0:T(8,128)S(1)} %get-tuple-element.60.pole_ref, f32[32,4096]{1,0:T(8,128)S(1)} %get-tuple-element.70.coef_ref), custom_call_target="tpu_custom_call" | custom-call | flops 2500000000 | bytes 1048576 | tf_op jit(solution)/shard_map/prepare/pallas_call | solution.py:548
  31.4 2.5 %prepare.3 = (f32[32,16,2048]{2,1,0:T(8,128)S(1)}, f32[8,32,2048]{2,1,0:T(8,128)S(1)}, f32[8,32,2048]{2,1,0:T(8,128)S(1)}) custom-call(s32[6]{0:T(128)S(1)} %copy-done.6, f32[8,32,2048]{2,1,0:T(8,128)S(1)} %get-tuple-element.93.e_ref, f32[32,4096]{1,0:T(8,128)S(1)} %get-tuple-element.60.pole_ref, f32[32,4096]{1,0:T(8,128)S(1)} %get-tuple-element.70.coef_ref), custom_call_target="tpu_custom_call" | custom-call | flops 2500000000 | bytes 1048576 | tf_op jit(solution)/shard_map/prepare/pallas_call | solution.py:548
  33.9 3.2 %collective-permute-done.4.met_ref = bf16[32,2048]{1,0:T(8,128)(2,1)S(1)} collective-permute-done((bf16[32,2048]{1,0:T(8,128)(2,1)S(1)}, bf16[32,2048]{1,0:T(8,128)(2,1)S(1)}, u32[]{:S(2)}, u32[]{:S(2)}) %collective-permute-start.4) | collective-permute-done | bytes 131104 | tf_op jit(solution)/shard_map/ppermute | solution.py:25
  37.1 0.2 round.5
  37.3 0.9 %collective-permute-start.5 = (bf16[32,2048]{1,0:T(8,128)(2,1)S(1)}, bf16[32,2048]{1,0:T(8,128)(2,1)S(1)}, u32[]{:S(2)}, u32[]{:S(2)}) collective-permute-start(bf16[32,2048]{1,0:T(8,128)(2,1)S(1)} %get-tuple-element.101), channel_id=1, source_target_pairs={{0,1},{1,0},{2,3},{3,2},{4,5},{5,4},{6,7},{7,6},{8,9},{9,8},{10,11... | collective-permute-start | bytes 393224 | tf_op jit(solution)/shard_map/ppermute | solution.py:25
  38.2 3.6 %back.2.refs_0_ = bf16[128,4096]{1,0:T(8,128)(2,1)} custom-call(f32[32,2048]{1,0:T(8,128)S(1)} %get-tuple-element.107.entry_ref, f32[32,16,2048]{2,1,0:T(8,128)S(1)} %get-tuple-element.108.table_ref, f32[8,32,2048]{2,1,0:T(8,128)S(1)} %get-tuple-element.109.local_ref, f32[8,32,2048]{2,1,0:T(8,128)S(1)} %get-tuple-element.110.reach_ref, ...), custom_call_target="tpu_custom_call" | custom-call | flops 3500000000 | bytes 1048576 | tf_op jit(solution)/shard_map/back/pallas_call | solution.py:597
  41.8 3.6 %back.3 = bf16[128,4096]{1,0:T(8,128)(2,1)} custom-call(bf16[32,2048]{1,0:T(8,128)(2,1)S(1)} %collective-permute-done.5.entry_ref, f32[32,16,2048]{2,1,0:T(8,128)S(1)} %get-tuple-element.102.table_ref, f32[8,32,2048]{2,1,0:T(8,128)S(1)} %get-tuple-element.103.local_ref, ...), custom_call_target="tpu_custom_call", output_to_operand_aliasing={{}: (6, {})} | custom-call | flops 3500000000 | bytes 1048576 | tf_op jit(solution)/shard_map/back/pallas_call | solution.py:597
  (17 shorter events, 0.0 us)
Async XLA Ops:
  1.0 5.5 %copy-start.1 = (f32[2,16,4096]{2,1,0:T(8,128)S(1)}, f32[2,16,4096]{2,1,0:T(8,128)}, u32[]{:S(2)}) copy-start(f32[2,16,4096]{2,1,0:T(8,128)} %residues_ref.1) | copy-start | bytes 1572868
  1.0 5.5 %copy-start.2 = (f32[16,4096]{1,0:T(8,128)S(1)}, f32[16,4096]{1,0:T(8,128)}, u32[]{:S(2)}) copy-start(f32[16,4096]{1,0:T(8,128)} %decay_ref.1) | copy-start | bytes 786436
  1.0 5.5 %copy-start.3 = (f32[16,4096]{1,0:T(8,128)S(1)}, f32[16,4096]{1,0:T(8,128)}, u32[]{:S(2)}) copy-start(f32[16,4096]{1,0:T(8,128)} %freq_ref.1) | copy-start | bytes 786436
  1.0 6.0 %copy-start.4 = (f32[3,3,4096]{2,1,0:T(4,128)S(1)}, f32[3,3,4096]{2,1,0:T(4,128)}, u32[]{:S(2)}) copy-start(f32[3,3,4096]{2,1,0:T(4,128)} %taps_ref.7) | copy-start | bytes 442372
  1.0 6.0 %collective-permute-start = (bf16[3,2,4096]{2,1,0:T(2,128)(2,1)S(1)}, bf16[3,2,4096]{2,1,0:T(2,128)(2,1)S(1)}, u32[]{:S(2)}, u32[]{:S(2)}) collective-permute-start(bf16[3,2,4096]{2,1,0:T(2,128)(2,1)S(1)} %slice.3), channel_id=1, source_target_pairs={{0,1},{1,2},{2,3},{3,4},{4,5},{5,6},{6,7},{7,8},{8,9},{9,10},{10,1... | collective-permute-start | bytes 147464 | tf_op jit(solution)/shard_map/ppermute | solution.py:539
  3.7 0.7 %copy-start.6 = (s32[6]{0:T(128)S(1)}, s32[6]{0:T(128)}, u32[]{:S(2)}) copy-start(s32[6]{0:T(128)} %lengths_ref.9) | copy-start | bytes 76
  11.3 5.6 %collective-permute-start.1 = (bf16[32,2048]{1,0:T(8,128)(2,1)S(1)}, bf16[32,2048]{1,0:T(8,128)(2,1)S(1)}, u32[]{:S(2)}, u32[]{:S(2)}) collective-permute-start(bf16[32,2048]{1,0:T(8,128)(2,1)S(1)} %get-tuple-element.65), channel_id=1, source_target_pairs={{0,1},{1,0},{2,3},{3,2},{4,5},{5,4},{6,7},{7,6},{8,9},{9,8},{10,11... | collective-permute-start | bytes 393224 | tf_op jit(solution)/shard_map/ppermute | solution.py:25
  12.7 4.6 %copy-start = (bf16[3,128,4096]{2,1,0:T(8,128)(2,1)S(1)}, bf16[3,128,4096]{2,1,0:T(8,128)(2,1)}, u32[]{:S(2)}) copy-start(bf16[3,128,4096]{2,1,0:T(8,128)(2,1)} %features_ref.5) | copy-start | bytes 9437188
  16.9 0.7 %copy-start.5 = (f32[4096]{0:T(1024)S(1)}, f32[4096]{0:T(1024)}, u32[]{:S(2)}) copy-start(f32[4096]{0:T(1024)} %param.9) | copy-start | bytes 49156
  17.2 5.5 %collective-permute-start.2 = (bf16[32,2048]{1,0:T(8,128)(2,1)S(1)}, bf16[32,2048]{1,0:T(8,128)(2,1)S(1)}, u32[]{:S(2)}, u32[]{:S(2)}) collective-permute-start(bf16[32,2048]{1,0:T(8,128)(2,1)S(1)} %get-tuple-element.67), channel_id=1, source_target_pairs={{0,2},{1,3},{2,0},{3,1},{4,6},{5,7},{6,4},{7,5},{8,10},{9,11},{10,... | collective-permute-start | bytes 393224 | tf_op jit(solution)/shard_map/ppermute | solution.py:25
  22.8 5.2 %collective-permute-start.3 = (bf16[32,2048]{1,0:T(8,128)(2,1)S(1)}, bf16[32,2048]{1,0:T(8,128)(2,1)S(1)}, u32[]{:S(2)}, u32[]{:S(2)}) collective-permute-start(bf16[32,2048]{1,0:T(8,128)(2,1)S(1)} %get-tuple-element.76), channel_id=1, source_target_pairs={{0,4},{1,5},{2,6},{3,7},{4,0},{5,1},{6,2},{7,3},{8,12},{9,13},{10,... | collective-permute-start | bytes 393224 | tf_op jit(solution)/shard_map/ppermute | solution.py:25
  28.3 8.8 %collective-permute-start.4 = (bf16[32,2048]{1,0:T(8,128)(2,1)S(1)}, bf16[32,2048]{1,0:T(8,128)(2,1)S(1)}, u32[]{:S(2)}, u32[]{:S(2)}) collective-permute-start(bf16[32,2048]{1,0:T(8,128)(2,1)S(1)} %get-tuple-element.86), channel_id=1, source_target_pairs={{0,8},{1,9},{2,10},{3,11},{4,12},{5,13},{6,14},{7,15},{8,0},{9,1},... | collective-permute-start | bytes 393224 | tf_op jit(solution)/shard_map/ppermute | solution.py:25
  37.3 4.5 %collective-permute-start.5 = (bf16[32,2048]{1,0:T(8,128)(2,1)S(1)}, bf16[32,2048]{1,0:T(8,128)(2,1)S(1)}, u32[]{:S(2)}, u32[]{:S(2)}) collective-permute-start(bf16[32,2048]{1,0:T(8,128)(2,1)S(1)} %get-tuple-element.101), channel_id=1, source_target_pairs={{0,1},{1,0},{2,3},{3,2},{4,5},{5,4},{6,7},{7,6},{8,9},{9,8},{10,11... | collective-permute-start | bytes 393224 | tf_op jit(solution)/shard_map/ppermute | solution.py:25
where the time goes:
time: 45.5 us; the launch traced here: 45.4 us
  Pallas kernels  34 us (75%)
  starting transfers between devices  5.9 us (13%)
  waiting for transfers between devices  3.24 us (7%)
  local copies, waits for them, and re-layouts  2 us (4%)
    pallas_call x12, Pallas kernels, call(): pl.pallas_call(body, grid_spec=pltpu.PrefetchScalarGridSpec(num_scalar_pr...  26.8 us
    pallas_call x2, Pallas kernels, back(): pl.pallas_call(functools.partial(back_kernel, mine=mine), in_specs=specs,...  7.19 us
    ppermute x5, waiting for transfers between devices, exchange(): return lax.ppermute(block, 'seq', [(i, i ^ distance) for i in devices])  3.23 us
    ppermute x5, starting transfers between devices, exchange(): return lax.ppermute(block, 'seq', [(i, i ^ distance) for i in devices])  3.22 us
    ppermute x1, starting transfers between devices, per_device(): halo = lax.ppermute(rim, 'seq', [(i, (i + 1) % n) for i in range(n)])  2.68 us
    unnamed x14, local copies, waits for them, and re-layouts  1.02 us
    slice x1, local copies, waits for them, and re-layouts, per_device(): rim = features[:, tokens - 2:, :]  0.98 us
  transfers between devices with their start and end apart: 6, of which 1 were waited for; matrix products, arithmetic and copies ran while one was open for 0% of the time, Pallas kernels for 56%

commit v1 on v0

--- a/solution.py
+++ b/solution.py
@@ -51,13 +51,11 @@
 def shift_matrix(starts, tokens):
     t = lax.broadcasted_iota(jnp.int32, (tokens, tokens), 0)
     u = lax.broadcasted_iota(jnp.int32, (tokens, tokens), 1)
-    here = jnp.zeros((tokens, tokens), jnp.bool_)
-    before = jnp.zeros((tokens, tokens), jnp.bool_)
+    last = jnp.full((tokens, tokens), -(1 << 30), jnp.int32)
     for s in starts:
-        here = here | (t == s)
-        before = before | (t - 1 == s)
-    one = jnp.where((u == t - 1) & ~here, 1.0, 0.0)
-    two = jnp.where((u == t - 2) & ~(here | before), 1.0, 0.0)
+        last = jnp.maximum(last, jnp.where(s <= t, s, -(1 << 30)))
+    one = jnp.where((u == t - 1) & (u >= last), 1.0, 0.0)
+    two = jnp.where((u == t - 2) & (u >= last), 1.0, 0.0)
     return jnp.concatenate([one, two], axis=0).astype(BF16)
 
 

time: 45.5 us -> 45 us (0.989); the launches traced: 45.4 us -> 44.4 us
  starting transfers between devices: 5.9 us -> 8.26 us
  Pallas kernels: 34 us -> 32.2 us
  waiting for transfers between devices: 3.24 us -> 1.7 us
    ppermute x5, starting transfers between devices: 3.22 us -> 5.58 us  [exchange(): return lax.ppermute(block, 'seq', [(i, i ^ distance) for i in devices])]
    pallas_call x12, Pallas kernels: 26.8 us -> 25 us  [call(): pl.pallas_call(body, grid_spec=pltpu.PrefetchScalarGridSpec(num_scalar_pr...]
    ppermute x5, waiting for transfers between devices: 3.23 us -> 1.7 us  [exchange(): return lax.ppermute(block, 'seq', [(i, i ^ distance) for i in devices])]
  transfers between devices with their start and end apart: 6 -> 6, of which waited for: 1 -> 2; matrix products, arithmetic and copies ran while one was open for 0% -> 0% of each run, Pallas kernels for 56% -> 53%
where the time goes in v1:
time: 45 us; the launch traced here: 44.4 us
  Pallas kernels  32.2 us (72%)
  starting transfers between devices  8.26 us (18%)
  local copies, waits for them, and re-layouts  2 us (4%)
  waiting for transfers between devices  1.7 us (4%)
    pallas_call x12, Pallas kernels, call(): pl.pallas_call(body, grid_spec=pltpu.PrefetchScalarGridSpec(num_scalar_pr...  25 us
    pallas_call x2, Pallas kernels, back(): pl.pallas_call(functools.partial(back_kernel, mine=mine), in_specs=specs,...  7.19 us
    ppermute x5, starting transfers between devices, exchange(): return lax.ppermute(block, 'seq', [(i, i ^ distance) for i in devices])  5.58 us
    ppermute x1, starting transfers between devices, per_device(): halo = lax.ppermute(rim, 'seq', [(i, (i + 1) % n) for i in range(n)])  2.68 us
    ppermute x5, waiting for transfers between devices, exchange(): return lax.ppermute(block, 'seq', [(i, i ^ distance) for i in devices])  1.7 us
    unnamed x14, local copies, waits for them, and re-layouts  1.02 us
    slice x1, local copies, waits for them, and re-layouts, per_device(): rim = features[:, tokens - 2:, :]  0.98 us
  transfers between devices with their start and end apart: 6, of which 2 were waited for; matrix products, arithmetic and copies ran while one was open for 0% of the time, Pallas kernels for 53%

profile of v1, /device:TPU:1, one launch (start us, length us, event | category | flops | bytes accessed | tf_op | source)
XLA Modules:
  0.0 44.4 jit_solution(227581944827203916)
XLA Ops:
  0.0 1.0 %slice.3 = bf16[3,2,4096]{2,1,0:T(2,128)(2,1)S(1)} slice(bf16[3,128,4096]{2,1,0:T(8,128)(2,1)} %features_ref.5), slice={[0:3], [126:128], [0:4096]} | slice | bytes 98304 | tf_op jit(solution)/shard_map/slice | solution.py:536
  1.0 2.7 %collective-permute-start = (bf16[3,2,4096]{2,1,0:T(2,128)(2,1)S(1)}, bf16[3,2,4096]{2,1,0:T(2,128)(2,1)S(1)}, u32[]{:S(2)}, u32[]{:S(2)}) collective-permute-start(bf16[3,2,4096]{2,1,0:T(2,128)(2,1)S(1)} %slice.3), channel_id=1, source_target_pairs={{0,1},{1,2},{2,3},{3,4},{4,5},{5,6},{6,7},{7,8},{8,9},{9,10},{10,1... | collective-permute-start | bytes 147464 | tf_op jit(solution)/shard_map/ppermute | solution.py:537
  3.7 0.7 %copy-done.6 = s32[6]{0:T(128)S(1)} copy-done((s32[6]{0:T(128)S(1)}, s32[6]{0:T(128)}, u32[]{:S(2)}) %copy-start.6) | copy-done | bytes 48
  4.4 2.1 %prelude.1 = (bf16[2,128,4096]{2,1,0:T(8,128)(2,1)S(1)}, bf16[256,128]{1,0:T(8,128)(2,1)S(1)}, f32[128,128]{1,0:T(8,128)S(1)}, f32[32,512]{1,0:T(8,128)S(1)}) custom-call(s32[6]{0:T(128)S(1)} %copy-done.6, bf16[3,128,4096]{2,1,0:T(8,128)(2,1)} %features_ref.5), custom_call_target="tpu_custom_call" | custom-call | flops 1200000000 | bytes 1048576 | tf_op jit(solution)/shard_map/prelude/pallas_call | solution.py:546
  6.5 0.5 %tables.1 = (f32[32,4096]{1,0:T(8,128)S(1)}, f32[32,4096]{1,0:T(8,128)S(1)}) custom-call(f32[16,4096]{1,0:T(8,128)S(1)} %copy-done.2, f32[16,4096]{1,0:T(8,128)S(1)} %copy-done.3, f32[2,16,4096]{2,1,0:T(8,128)S(1)} %copy-done.1), custom_call_target="tpu_custom_call" | custom-call | flops 500000000 | bytes 1048576 | tf_op jit(solution)/shard_map/tables/pallas_call | solution.py:546
  7.0 4.2 %front.3 = (bf16[128,2048]{1,0:T(8,128)(2,1)S(1)}, f32[8,32,2048]{2,1,0:T(8,128)S(1)}, bf16[32,2048]{1,0:T(8,128)(2,1)S(1)}) custom-call(bf16[2,128,4096]{2,1,0:T(8,128)(2,1)S(1)} %get-tuple-element.59.streams_ref, bf16[3,2,4096]{2,1,0:T(2,128)(2,1)S(1)} %collective-permute-done.halo_ref, f32[3,3,4096]{2,1,0:T(4,128)S(1)} %copy-done.4, ...), custom_call_target="tpu_custom_call" | custom-call | flops 5000000000 | bytes 1048576 | tf_op jit(solution)/shard_map/front/pallas_call | solution.py:546
  11.3 1.4 %collective-permute-start.1 = (bf16[32,2048]{1,0:T(8,128)(2,1)S(1)}, bf16[32,2048]{1,0:T(8,128)(2,1)S(1)}, u32[]{:S(2)}, u32[]{:S(2)}) collective-permute-start(bf16[32,2048]{1,0:T(8,128)(2,1)S(1)} %get-tuple-element.65), channel_id=1, source_target_pairs={{0,1},{1,0},{2,3},{3,2},{4,5},{5,4},{6,7},{7,6},{8,9},{9,8},{10,11... | collective-permute-start | bytes 393224 | tf_op jit(solution)/shard_map/ppermute | solution.py:25
  12.7 4.2 %front.2 = (bf16[128,2048]{1,0:T(8,128)(2,1)S(1)}, f32[8,32,2048]{2,1,0:T(8,128)S(1)}, bf16[32,2048]{1,0:T(8,128)(2,1)S(1)}) custom-call(bf16[2,128,4096]{2,1,0:T(8,128)(2,1)S(1)} %get-tuple-element.59.streams_ref, bf16[3,2,4096]{2,1,0:T(2,128)(2,1)S(1)} %collective-permute-done.halo_ref, f32[3,3,4096]{2,1,0:T(4,128)S(1)} %copy-done.4, ...), custom_call_target="tpu_custom_call" | custom-call | flops 5000000000 | bytes 1048576 | tf_op jit(solution)/shard_map/front/pallas_call | solution.py:546
  16.9 0.3 first.1
  17.3 0.3 copy-done.5
  17.6 4.1 %middle.2 = (f32[128,2048]{1,0:T(8,128)S(1)}, f32[128,2048]{1,0:T(8,128)S(1)}) custom-call(s32[6]{0:T(128)S(1)} %copy-done.6, bf16[3,128,4096]{2,1,0:T(8,128)(2,1)S(1)} %copy-done, bf16[3,2,4096]{2,1,0:T(2,128)(2,1)S(1)} %collective-permute-done.halo_ref, f32[3,3,4096]{2,1,0:T(4,128)S(1)} %copy-done.4, bf16[128,2048]{1,0:T(8,128)(2,1)S(1)} %get-tuple-element.69.z_ref, ...), custom_call_target="tpu_custom_call" | custom-call | flops 5000000000 | bytes 1048576 | tf_op jit(solution)/shard_map/middle/pallas_call | solution.py:546
  21.8 0.6 %collective-permute-done.2.met_ref = bf16[32,2048]{1,0:T(8,128)(2,1)S(1)} collective-permute-done((bf16[32,2048]{1,0:T(8,128)(2,1)S(1)}, bf16[32,2048]{1,0:T(8,128)(2,1)S(1)}, u32[]{:S(2)}, u32[]{:S(2)}) %collective-permute-start.2) | collective-permute-done | bytes 131104 | tf_op jit(solution)/shard_map/ppermute | solution.py:25
  22.3 0.2 round.3
  22.5 0.4 collective-permute-start.3
  22.9 4.1 %middle.3 = (f32[128,2048]{1,0:T(8,128)S(1)}, f32[128,2048]{1,0:T(8,128)S(1)}) custom-call(s32[6]{0:T(128)S(1)} %copy-done.6, bf16[3,128,4096]{2,1,0:T(8,128)(2,1)S(1)} %copy-done, bf16[3,2,4096]{2,1,0:T(2,128)(2,1)S(1)} %collective-permute-done.halo_ref, f32[3,3,4096]{2,1,0:T(4,128)S(1)} %copy-done.4, bf16[128,2048]{1,0:T(8,128)(2,1)S(1)} %get-tuple-element.78.z_ref, ...), custom_call_target="tpu_custom_call" | custom-call | flops 5000000000 | bytes 1048576 | tf_op jit(solution)/shard_map/middle/pallas_call | solution.py:546
  27.1 0.2 round.4
  27.3 2.2 %collective-permute-start.4 = (bf16[32,2048]{1,0:T(8,128)(2,1)S(1)}, bf16[32,2048]{1,0:T(8,128)(2,1)S(1)}, u32[]{:S(2)}, u32[]{:S(2)}) collective-permute-start(bf16[32,2048]{1,0:T(8,128)(2,1)S(1)} %get-tuple-element.86), channel_id=1, source_target_pairs={{0,8},{1,9},{2,10},{3,11},{4,12},{5,13},{6,14},{7,15},{8,0},{9,1},... | collective-permute-start | bytes 393224 | tf_op jit(solution)/shard_map/ppermute | solution.py:25
  29.5 2.5 %prepare.2 = (f32[32,16,2048]{2,1,0:T(8,128)S(1)}, f32[8,32,2048]{2,1,0:T(8,128)S(1)}, f32[8,32,2048]{2,1,0:T(8,128)S(1)}) custom-call(s32[6]{0:T(128)S(1)} %copy-done.6, f32[8,32,2048]{2,1,0:T(8,128)S(1)} %get-tuple-element.89.e_ref, f32[32,4096]{1,0:T(8,128)S(1)} %get-tuple-element.60.pole_ref, f32[32,4096]{1,0:T(8,128)S(1)} %get-tuple-element.70.coef_ref), custom_call_target="tpu_custom_call" | custom-call | flops 2500000000 | bytes 1048576 | tf_op jit(solution)/shard_map/prepare/pallas_call | solution.py:546
  32.0 2.5 %prepare.3 = (f32[32,16,2048]{2,1,0:T(8,128)S(1)}, f32[8,32,2048]{2,1,0:T(8,128)S(1)}, f32[8,32,2048]{2,1,0:T(8,128)S(1)}) custom-call(s32[6]{0:T(128)S(1)} %copy-done.6, f32[8,32,2048]{2,1,0:T(8,128)S(1)} %get-tuple-element.93.e_ref, f32[32,4096]{1,0:T(8,128)S(1)} %get-tuple-element.60.pole_ref, f32[32,4096]{1,0:T(8,128)S(1)} %get-tuple-element.70.coef_ref), custom_call_target="tpu_custom_call" | custom-call | flops 2500000000 | bytes 1048576 | tf_op jit(solution)/shard_map/prepare/pallas_call | solution.py:546
  34.4 1.1 %collective-permute-done.4.met_ref = bf16[32,2048]{1,0:T(8,128)(2,1)S(1)} collective-permute-done((bf16[32,2048]{1,0:T(8,128)(2,1)S(1)}, bf16[32,2048]{1,0:T(8,128)(2,1)S(1)}, u32[]{:S(2)}, u32[]{:S(2)}) %collective-permute-start.4) | collective-permute-done | bytes 131104 | tf_op jit(solution)/shard_map/ppermute | solution.py:25
  35.5 0.2 round.5
  35.7 1.5 %collective-permute-start.5 = (bf16[32,2048]{1,0:T(8,128)(2,1)S(1)}, bf16[32,2048]{1,0:T(8,128)(2,1)S(1)}, u32[]{:S(2)}, u32[]{:S(2)}) collective-permute-start(bf16[32,2048]{1,0:T(8,128)(2,1)S(1)} %get-tuple-element.101), channel_id=1, source_target_pairs={{0,1},{1,0},{2,3},{3,2},{4,5},{5,4},{6,7},{7,6},{8,9},{9,8},{10,11... | collective-permute-start | bytes 393224 | tf_op jit(solution)/shard_map/ppermute | solution.py:25
  37.2 3.6 %back.2.refs_0_ = bf16[128,4096]{1,0:T(8,128)(2,1)} custom-call(f32[32,2048]{1,0:T(8,128)S(1)} %get-tuple-element.107.entry_ref, f32[32,16,2048]{2,1,0:T(8,128)S(1)} %get-tuple-element.108.table_ref, f32[8,32,2048]{2,1,0:T(8,128)S(1)} %get-tuple-element.109.local_ref, f32[8,32,2048]{2,1,0:T(8,128)S(1)} %get-tuple-element.110.reach_ref, ...), custom_call_target="tpu_custom_call" | custom-call | flops 3500000000 | bytes 1048576 | tf_op jit(solution)/shard_map/back/pallas_call | solution.py:595
  40.8 3.6 %back.3 = bf16[128,4096]{1,0:T(8,128)(2,1)} custom-call(bf16[32,2048]{1,0:T(8,128)(2,1)S(1)} %collective-permute-done.5.entry_ref, f32[32,16,2048]{2,1,0:T(8,128)S(1)} %get-tuple-element.102.table_ref, f32[8,32,2048]{2,1,0:T(8,128)S(1)} %get-tuple-element.103.local_ref, ...), custom_call_target="tpu_custom_call", output_to_operand_aliasing={{}: (6, {})} | custom-call | flops 3500000000 | bytes 1048576 | tf_op jit(solution)/shard_map/back/pallas_call | solution.py:595
  (17 shorter events, 0.1 us)
Async XLA Ops:
  1.0 5.5 %copy-start.1 = (f32[2,16,4096]{2,1,0:T(8,128)S(1)}, f32[2,16,4096]{2,1,0:T(8,128)}, u32[]{:S(2)}) copy-start(f32[2,16,4096]{2,1,0:T(8,128)} %residues_ref.1) | copy-start | bytes 1572868
  1.0 5.5 %copy-start.2 = (f32[16,4096]{1,0:T(8,128)S(1)}, f32[16,4096]{1,0:T(8,128)}, u32[]{:S(2)}) copy-start(f32[16,4096]{1,0:T(8,128)} %decay_ref.1) | copy-start | bytes 786436
  1.0 5.5 %copy-start.3 = (f32[16,4096]{1,0:T(8,128)S(1)}, f32[16,4096]{1,0:T(8,128)}, u32[]{:S(2)}) copy-start(f32[16,4096]{1,0:T(8,128)} %freq_ref.1) | copy-start | bytes 786436
  1.0 6.0 %copy-start.4 = (f32[3,3,4096]{2,1,0:T(4,128)S(1)}, f32[3,3,4096]{2,1,0:T(4,128)}, u32[]{:S(2)}) copy-start(f32[3,3,4096]{2,1,0:T(4,128)} %taps_ref.7) | copy-start | bytes 442372
  1.0 6.0 %collective-permute-start = (bf16[3,2,4096]{2,1,0:T(2,128)(2,1)S(1)}, bf16[3,2,4096]{2,1,0:T(2,128)(2,1)S(1)}, u32[]{:S(2)}, u32[]{:S(2)}) collective-permute-start(bf16[3,2,4096]{2,1,0:T(2,128)(2,1)S(1)} %slice.3), channel_id=1, source_target_pairs={{0,1},{1,2},{2,3},{3,4},{4,5},{5,6},{6,7},{7,8},{8,9},{9,10},{10,1... | collective-permute-start | bytes 147464 | tf_op jit(solution)/shard_map/ppermute | solution.py:537
  3.7 0.7 %copy-start.6 = (s32[6]{0:T(128)S(1)}, s32[6]{0:T(128)}, u32[]{:S(2)}) copy-start(s32[6]{0:T(128)} %lengths_ref.9) | copy-start | bytes 76
  11.3 5.6 %collective-permute-start.1 = (bf16[32,2048]{1,0:T(8,128)(2,1)S(1)}, bf16[32,2048]{1,0:T(8,128)(2,1)S(1)}, u32[]{:S(2)}, u32[]{:S(2)}) collective-permute-start(bf16[32,2048]{1,0:T(8,128)(2,1)S(1)} %get-tuple-element.65), channel_id=1, source_target_pairs={{0,1},{1,0},{2,3},{3,2},{4,5},{5,4},{6,7},{7,6},{8,9},{9,8},{10,11... | collective-permute-start | bytes 393224 | tf_op jit(solution)/shard_map/ppermute | solution.py:25
  12.7 4.6 %copy-start = (bf16[3,128,4096]{2,1,0:T(8,128)(2,1)S(1)}, bf16[3,128,4096]{2,1,0:T(8,128)(2,1)}, u32[]{:S(2)}) copy-start(bf16[3,128,4096]{2,1,0:T(8,128)(2,1)} %features_ref.5) | copy-start | bytes 9437188
  16.9 0.7 %copy-start.5 = (f32[4096]{0:T(1024)S(1)}, f32[4096]{0:T(1024)}, u32[]{:S(2)}) copy-start(f32[4096]{0:T(1024)} %param.9) | copy-start | bytes 49156
  17.2 5.2 %collective-permute-start.2 = (bf16[32,2048]{1,0:T(8,128)(2,1)S(1)}, bf16[32,2048]{1,0:T(8,128)(2,1)S(1)}, u32[]{:S(2)}, u32[]{:S(2)}) collective-permute-start(bf16[32,2048]{1,0:T(8,128)(2,1)S(1)} %get-tuple-element.67), channel_id=1, source_target_pairs={{0,2},{1,3},{2,0},{3,1},{4,6},{5,7},{6,4},{7,5},{8,10},{9,11},{10,... | collective-permute-start | bytes 393224 | tf_op jit(solution)/shard_map/ppermute | solution.py:25
  22.5 4.5 %collective-permute-start.3 = (bf16[32,2048]{1,0:T(8,128)(2,1)S(1)}, bf16[32,2048]{1,0:T(8,128)(2,1)S(1)}, u32[]{:S(2)}, u32[]{:S(2)}) collective-permute-start(bf16[32,2048]{1,0:T(8,128)(2,1)S(1)} %get-tuple-element.76), channel_id=1, source_target_pairs={{0,4},{1,5},{2,6},{3,7},{4,0},{5,1},{6,2},{7,3},{8,12},{9,13},{10,... | collective-permute-start | bytes 393224 | tf_op jit(solution)/shard_map/ppermute | solution.py:25
  27.3 8.3 %collective-permute-start.4 = (bf16[32,2048]{1,0:T(8,128)(2,1)S(1)}, bf16[32,2048]{1,0:T(8,128)(2,1)S(1)}, u32[]{:S(2)}, u32[]{:S(2)}) collective-permute-start(bf16[32,2048]{1,0:T(8,128)(2,1)S(1)} %get-tuple-element.86), channel_id=1, source_target_pairs={{0,8},{1,9},{2,10},{3,11},{4,12},{5,13},{6,14},{7,15},{8,0},{9,1},... | collective-permute-start | bytes 393224 | tf_op jit(solution)/shard_map/ppermute | solution.py:25
  35.7 5.1 %collective-permute-start.5 = (bf16[32,2048]{1,0:T(8,128)(2,1)S(1)}, bf16[32,2048]{1,0:T(8,128)(2,1)S(1)}, u32[]{:S(2)}, u32[]{:S(2)}) collective-permute-start(bf16[32,2048]{1,0:T(8,128)(2,1)S(1)} %get-tuple-element.101), channel_id=1, source_target_pairs={{0,1},{1,0},{2,3},{3,2},{4,5},{5,4},{6,7},{7,6},{8,9},{9,8},{10,11... | collective-permute-start | bytes 393224 | tf_op jit(solution)/shard_map/ppermute | solution.py:25
